TPU v7x, 256 devices: a whole 4x4x8 slice. The times are simulated.
256 devices in a mesh: dp: 4 (over y), cp: 64 (over x, z, core).
Axes of the slice: x: 4, y: 4, z: 8, core: 2. Of those that a mesh axis runs over, the one named last changes fastest.
Arguments:
- query_rows: bfloat16 [32768, 4096], P(('dp', 'cp')), parts along dimension 0, may hold values from -90 to 90
- key_rows: bfloat16 [32768, 512], P(('dp', 'cp')), parts along dimension 0, may hold values from -5 to 5
- value_rows: bfloat16 [32768, 512], P(('dp', 'cp')), parts along dimension 0, may hold values from -6 to 6
- gate_rows: bfloat16 [32768, 4096], P(('dp', 'cp')), parts along dimension 0, may hold values from -6 to 6
- doc_ids: int32 [32768], P(('dp', 'cp')), parts along dimension 0, may hold values from 0 to 15, never falling along the last dimension, each value on 1 to 4096 neighbouring positions
- block_lists: int32 [256, 64], P(('dp', 'cp')), parts along dimension 0, may hold values from 0 to 1, as said below
Outputs:
- gated_attention: bfloat16 [32768, 4096], P(('dp', 'cp')), parts along dimension 0
There are 4 independent parts, one for each index of `dp`. A program takes and returns all parts, laid end to end along the dimension named above; each array names one. Nothing has to cross between parts.
Inputs may be any that keep to these rules, and one draw needn't show every extreme that they name: `block_lists`: row q has a 1 at column q and only zeros at columns above q.
All inputs are finite; a program needn't handle non-finite values.
Results may differ from a plain program's by a relative error of at most 0.0038.
Values may be sent and summed in bfloat16 or wider, within the bound.
No kernel may reach another device: no remote copies, remote signals or barrier semaphores. Data moves between devices by JAX's collectives and lax.ppermute only.
A program may use at most 128 MiB of HBM per device.

v0:
```python
import math
import jax
import jax.numpy as jnp
from jax import lax
from jax.sharding import PartitionSpec as P

H = 16
KVH = 2
HD = 256
BLK = 128


def pick_size(length):
    for candidate in (2048, 1024, 512, 256, 128):
        return candidate
    return length


def make_fold(query_rows, positions, query_docs, all_docs, all_lists):
    total_rows = query_rows.shape[0]
    num_blocks = all_lists.shape[0]
    seq_rows = all_docs.shape[0]
    groups = H // KVH
    scale_factor = 1.0 / math.sqrt(HD)
    grouped = query_rows.reshape(total_rows, KVH, groups, HD)
    block_range = jnp.arange(num_blocks, dtype=jnp.int32)
    selector = ((positions // BLK)[:, None] == block_range[None, :]).astype(jnp.bfloat16)
    row_lists = jnp.dot(
        selector, all_lists.astype(jnp.bfloat16), preferred_element_type=jnp.float32
    ).astype(jnp.bfloat16)
    padded_lists = jnp.concatenate(
        [jnp.zeros((total_rows, num_blocks), jnp.bfloat16), row_lists], axis=1
    )
    padded_docs = jnp.concatenate([jnp.full((seq_rows,), -1, jnp.int32), all_docs], axis=0)

    def update(state, key_block, value_block, block_start):
        width = key_block.shape[0]
        key_pos = block_start + jnp.arange(width, dtype=jnp.int32)
        key_docs = lax.dynamic_slice_in_dim(padded_docs, block_start + seq_rows, width)
        block_count = width // BLK
        listed_blocks = lax.dynamic_slice_in_dim(
            padded_lists, block_start // BLK + num_blocks, block_count, 1
        )
        listed = jnp.repeat(listed_blocks, BLK, axis=1)
        visible = (
            (key_pos[None, :] >= 0)
            & (key_pos[None, :] <= positions[:, None])
            & (key_docs[None, :] == query_docs[:, None])
            & (listed > 0.5)
        )

        def compute(inner):
            running_max, running_sum, weighted = inner
            scores = (
                jnp.einsum(
                    "rkgd,nkd->kgrn",
                    grouped,
                    key_block.reshape(width, KVH, HD),
                    preferred_element_type=jnp.float32,
                )
                * scale_factor
            )
            scores = jnp.where(visible[None, None], scores, -1e30)
            new_max = jnp.maximum(running_max, jnp.max(scores, axis=-1))
            weights = jnp.where(visible[None, None], jnp.exp(scores - new_max[..., None]), 0.0)
            decay = jnp.exp(running_max - new_max)
            new_sum = decay * running_sum + jnp.sum(weights, axis=-1)
            product = jnp.einsum(
                "kgrn,nkd->kgrd",
                weights.astype(jnp.bfloat16),
                value_block.reshape(width, KVH, HD),
                preferred_element_type=jnp.float32,
            )
            return (new_max, new_sum, decay[..., None] * weighted + product)

        return lax.cond(jnp.any(visible), compute, lambda inner: inner, state)

    def fold(state, piece, start):
        key_piece, value_piece = piece
        length = key_piece.shape[0]
        step_size = pick_size(length)
        count = length // step_size
        key_steps = key_piece.reshape(count, step_size, key_piece.shape[1])
        value_steps = value_piece.reshape(count, step_size, value_piece.shape[1])
        starts = step_size * jnp.arange(count, dtype=jnp.int32)

        def advance(inner, inputs):
            return (update(inner, inputs[0], inputs[1], inputs[2]), None)

        state, _ = lax.scan(advance, state, (key_steps, value_steps, starts))
        return state

    initial = (
        jnp.full((KVH, groups, total_rows), -1e30, jnp.float32),
        jnp.zeros((KVH, groups, total_rows), jnp.float32),
        jnp.zeros((KVH, groups, total_rows, HD), jnp.float32),
    )
    return (fold, initial)


def finish(state, total_rows):
    running_max, running_sum, weighted = state
    result = weighted / running_sum[..., None]
    return jnp.transpose(result, (2, 0, 1, 3)).reshape(total_rows, H * HD)


def fold_all(fold, initial, key_rows, value_rows):
    return fold(
        initial,
        (
            lax.all_gather(key_rows, "cp", axis=0, tiled=True),
            lax.all_gather(value_rows, "cp", axis=0, tiled=True),
        ),
        jnp.int32(0),
    )


def on_device(query_rows, key_rows, value_rows, gate_rows, doc_ids, block_lists):
    rows_here = query_rows.shape[0]
    position = lax.axis_index("cp")
    all_docs, all_lists = (
        lax.all_gather(doc_ids, "cp", axis=0, tiled=True),
        lax.all_gather(block_lists, "cp", axis=0, tiled=True),
    )
    first_row = position * rows_here
    positions = first_row + jnp.arange(rows_here, dtype=jnp.int32)
    fold, initial = make_fold(query_rows, positions, doc_ids, all_docs, all_lists)
    state = fold_all(fold, initial, key_rows, value_rows)
    attended = finish(state, rows_here)
    gated = (attended * jax.nn.sigmoid(gate_rows.astype(jnp.float32))).astype(jnp.bfloat16)
    return gated


def solution(mesh):
    return jax.shard_map(
        on_device,
        mesh=mesh,
        in_specs=(
            P(("dp", "cp"), None),
            P(("dp", "cp"), None),
            P(("dp", "cp"), None),
            P(("dp", "cp"), None),
            P(("dp", "cp")),
            P(("dp", "cp"), None),
        ),
        out_specs=P(("dp", "cp"), None),
        check_vma=False,
    )
```

profile of v0, /device:TPU:7, one launch (start us, length us, event | category | flops | bytes accessed | tf_op | source)
XLA Modules:
  0.0 298.2 jit_solution(7128368392556407107)
XLA Ops:
  8.0 1.6 copy.41
  11.0 41.3 %all-gather.1 = s32[64,1,64]{2,1,0:T(1,128)S(1)} all-gather(s32[1,1,64]{2,1,0:T(1,128)S(1)} %bitcast.63), channel_id=1, replica_groups=mesh['dp'=4,'cp'=64] {'cp'}, dimensions={0}, use_global_device_ids=true | all-gather | bytes 16640 | tf_op jit(solution)/shard_map/all_gather | solution.py:123
  52.5 37.4 %all-gather = s32[64,1,128]{2,1,0:T(1,128)S(1)} all-gather(s32[1,1,128]{2,1,0:T(1,128)S(1)} %bitcast.61), channel_id=1, replica_groups=mesh['dp'=4,'cp'=64] {'cp'}, dimensions={0}, use_global_device_ids=true | all-gather | bytes 33280 | tf_op jit(solution)/shard_map/all_gather | solution.py:122
  90.0 4.8 %all-gather.5.cloned.1.call-done = bf16[8192,512]{1,0:T(8,128)(2,1)} async-done(((bf16[128,512]{1,0:T(8,128)(2,1)}), bf16[8192,512]{1,0:T(8,128)(2,1)}) %all-gather.5.cloned.1.call-update) | async-done | bytes 8388624 | tf_op jit(solution)/shard_map/all_gather | solution.py:111
  94.7 11.5 %copy.42 = bf16[4,2048,512]{1,2,0:T(8,128)(2,1)} copy(bf16[4,2048,512]{2,1,0:T(8,128)(2,1)} %bitcast.54) | data formatting | bytes 16777216
  106.2 71.6 %all-gather.7.cloned.1.call-done = bf16[8192,512]{1,0:T(8,128)(2,1)} async-done(((bf16[128,512]{1,0:T(8,128)(2,1)}), bf16[8192,512]{1,0:T(8,128)(2,1)}) %all-gather.7.cloned.1.call-update) | async-done | bytes 8388624 | tf_op jit(solution)/shard_map/all_gather | solution.py:112
  177.8 11.4 %copy.44 = bf16[4,2048,512]{1,2,0:T(8,128)(2,1)} copy(bf16[4,2048,512]{2,1,0:T(8,128)(2,1)} %bitcast.55) | data formatting | bytes 16777216
  189.3 1.6 broadcast_in_dim.58
  190.9 96.7 %while.17 = (s32[]{:T(128)}, f32[2,8,128]{2,1,0:T(8,128)S(1)}, f32[2,8,128]{2,1,0:T(8,128)S(1)}, f32[2,8,128,256]{3,2,1,0:T(8,128)}, s32[4]{0:T(128)S(1)}, /*ind...) while((s32[]{:T(128)}, f32[2,8,128]{2,1,0:T(8,128)S(1)}, ...), condition=%wide.region_6.7_spmd.clone, body=%wide.region_0.6_spmd.clone.sunk | while | flops 4353456128 | bytes 73665688 | solution.py:90
  197.3 1.4 and_reduce_fusion.2
  207.9 20.9 %conditional.3 = ((f32[2,8,128]{2,1,0:T(8,128)S(1)}, f32[2,8,128]{2,1,0:T(8,128)S(1)}, f32[2,8,128,256]{3,2,1,0:T(8,128)})) conditional(s32[]{:T(128)} %convert_element_type.42, (f32[2,8,128]{2,1,0:T(8,128)S(1)}, f32[2,8,128]{2,1,0:T(8,128)S(1)}, f32[2,8,128,256]{3,2,1,0:T(8,128)}) %tuple.57, (s32[]{:T(128)}, s32[1,2048]{1,0:T(1,128)S(1)}, ...), branch_computations={%region_2.2_spmd, %region_3.5_spmd} | conditional | flops 4351862784 | bytes 73577536 | solution.py:76
  208.6 1.8 bitcast_and_fusion
  210.4 2.7 constant_dynamic-slice_fusion
  213.2 4.0 %fusion.2 = (f32[2,8,128]{2,1,0:T(8,128)S(1)}, f32[2,2048,128,8]{2,1,3,0:T(8,128)S(1)}) fusion(pred[128,2048]{0,1:T(8,128)(4,1)S(1)} %bitcast_and_fusion, bf16[2048,2,256,1]{0,2,3,1:T(8,128)(2,1)S(1)} %bitcast.53, bf16[128,2,8,256]{3,0,2,1:T(8,128)(2,1)S(1)} %copy-done), kind=kOutput, calls=%fused_computation.3 | convolution fusion | flops 2160064512 | bytes 20193280 | tf_op jit(solution)/shard_map/while/body/eval_jaxpr/cond/branch_1_fun/rkgd,nkd->kgrn/dot_general | solution.py:55
  217.1 4.0 %fusion.4 = f32[2,8,128]{2,1,0:T(8,128)S(1)} fusion(f32[2,2048,128,8]{2,1,3,0:T(8,128)S(1)} %get-tuple-element.413, f32[2,8,128]{2,1,0:T(8,128)S(1)} %max.4, pred[128,2048]{0,1:T(8,128)(4,1)S(1)} %bitcast_and_fusion), kind=kLoop, calls=%fused_computation.5 | loop fusion | flops 20969472 | bytes 17055744 | tf_op jit(solution)/shard_map/while/body/eval_jaxpr/cond/branch_1_fun/reduce_sum | solution.py:67
  221.1 7.6 %multiply_add_fusion = f32[2,8,128,256]{3,2,1,0:T(8,128)} fusion(f32[2,8,128,256]{3,2,1,0:T(8,128)} %get-tuple-element.282, bf16[2048,2,256,1]{0,2,3,1:T(8,128)(2,1)S(1)} %bitcast.52, f32[2,2048,128,8]{2,1,3,0:T(8,128)S(1)} %get-tuple-element.413, f32[2,8,128]{2,1,0:T(8,128)S(1)} %max.4, pred[128,2048]{0,1:T(8,128)(4,1)S(1)} %bitcast_and_fusion, ...), kind=kOutput, calls=%fused_computation.8 | convolution fusion | flops 2169503744 | bytes 23347200 | tf_op jit(solution)/shard_map/while/body/eval_jaxpr/cond/branch_1_fun/kgrn,nkd->kgrd/dot_general | solution.py:68
  235.2 1.4 and_reduce_fusion.2
  237.3 20.9 %conditional.3 = ((f32[2,8,128]{2,1,0:T(8,128)S(1)}, f32[2,8,128]{2,1,0:T(8,128)S(1)}, f32[2,8,128,256]{3,2,1,0:T(8,128)})) conditional(s32[]{:T(128)} %convert_element_type.42, (f32[2,8,128]{2,1,0:T(8,128)S(1)}, f32[2,8,128]{2,1,0:T(8,128)S(1)}, f32[2,8,128,256]{3,2,1,0:T(8,128)}) %tuple.57, (s32[]{:T(128)}, s32[1,2048]{1,0:T(1,128)S(1)}, ...), branch_computations={%region_2.2_spmd, %region_3.5_spmd} | conditional | flops 4351862784 | bytes 73577536 | solution.py:76
  238.0 1.8 bitcast_and_fusion
  239.8 2.7 constant_dynamic-slice_fusion
  242.6 4.0 %fusion.2 = (f32[2,8,128]{2,1,0:T(8,128)S(1)}, f32[2,2048,128,8]{2,1,3,0:T(8,128)S(1)}) fusion(pred[128,2048]{0,1:T(8,128)(4,1)S(1)} %bitcast_and_fusion, bf16[2048,2,256,1]{0,2,3,1:T(8,128)(2,1)S(1)} %bitcast.53, bf16[128,2,8,256]{3,0,2,1:T(8,128)(2,1)S(1)} %copy-done), kind=kOutput, calls=%fused_computation.3 | convolution fusion | flops 2160064512 | bytes 20193280 | tf_op jit(solution)/shard_map/while/body/eval_jaxpr/cond/branch_1_fun/rkgd,nkd->kgrn/dot_general | solution.py:55
  246.5 4.0 %fusion.4 = f32[2,8,128]{2,1,0:T(8,128)S(1)} fusion(f32[2,2048,128,8]{2,1,3,0:T(8,128)S(1)} %get-tuple-element.413, f32[2,8,128]{2,1,0:T(8,128)S(1)} %max.4, pred[128,2048]{0,1:T(8,128)(4,1)S(1)} %bitcast_and_fusion), kind=kLoop, calls=%fused_computation.5 | loop fusion | flops 20969472 | bytes 17055744 | tf_op jit(solution)/shard_map/while/body/eval_jaxpr/cond/branch_1_fun/reduce_sum | solution.py:67
  250.5 7.6 %multiply_add_fusion = f32[2,8,128,256]{3,2,1,0:T(8,128)} fusion(f32[2,8,128,256]{3,2,1,0:T(8,128)} %get-tuple-element.282, bf16[2048,2,256,1]{0,2,3,1:T(8,128)(2,1)S(1)} %bitcast.52, f32[2,2048,128,8]{2,1,3,0:T(8,128)S(1)} %get-tuple-element.413, f32[2,8,128]{2,1,0:T(8,128)S(1)} %max.4, pred[128,2048]{0,1:T(8,128)(4,1)S(1)} %bitcast_and_fusion, ...), kind=kOutput, calls=%fused_computation.8 | convolution fusion | flops 2169503744 | bytes 23347200 | tf_op jit(solution)/shard_map/while/body/eval_jaxpr/cond/branch_1_fun/kgrn,nkd->kgrd/dot_general | solution.py:68
  264.6 1.4 and_reduce_fusion.2
  266.7 20.9 %conditional.3 = ((f32[2,8,128]{2,1,0:T(8,128)S(1)}, f32[2,8,128]{2,1,0:T(8,128)S(1)}, f32[2,8,128,256]{3,2,1,0:T(8,128)})) conditional(s32[]{:T(128)} %convert_element_type.42, (f32[2,8,128]{2,1,0:T(8,128)S(1)}, f32[2,8,128]{2,1,0:T(8,128)S(1)}, f32[2,8,128,256]{3,2,1,0:T(8,128)}) %tuple.57, (s32[]{:T(128)}, s32[1,2048]{1,0:T(1,128)S(1)}, ...), branch_computations={%region_2.2_spmd, %region_3.5_spmd} | conditional | flops 4351862784 | bytes 73577536 | solution.py:76
  267.4 1.8 bitcast_and_fusion
  269.2 2.7 constant_dynamic-slice_fusion
  272.0 4.0 %fusion.2 = (f32[2,8,128]{2,1,0:T(8,128)S(1)}, f32[2,2048,128,8]{2,1,3,0:T(8,128)S(1)}) fusion(pred[128,2048]{0,1:T(8,128)(4,1)S(1)} %bitcast_and_fusion, bf16[2048,2,256,1]{0,2,3,1:T(8,128)(2,1)S(1)} %bitcast.53, bf16[128,2,8,256]{3,0,2,1:T(8,128)(2,1)S(1)} %copy-done), kind=kOutput, calls=%fused_computation.3 | convolution fusion | flops 2160064512 | bytes 20193280 | tf_op jit(solution)/shard_map/while/body/eval_jaxpr/cond/branch_1_fun/rkgd,nkd->kgrn/dot_general | solution.py:55
  275.9 4.0 %fusion.4 = f32[2,8,128]{2,1,0:T(8,128)S(1)} fusion(f32[2,2048,128,8]{2,1,3,0:T(8,128)S(1)} %get-tuple-element.413, f32[2,8,128]{2,1,0:T(8,128)S(1)} %max.4, pred[128,2048]{0,1:T(8,128)(4,1)S(1)} %bitcast_and_fusion), kind=kLoop, calls=%fused_computation.5 | loop fusion | flops 20969472 | bytes 17055744 | tf_op jit(solution)/shard_map/while/body/eval_jaxpr/cond/branch_1_fun/reduce_sum | solution.py:67
  279.9 7.6 %multiply_add_fusion = f32[2,8,128,256]{3,2,1,0:T(8,128)} fusion(f32[2,8,128,256]{3,2,1,0:T(8,128)} %get-tuple-element.282, bf16[2048,2,256,1]{0,2,3,1:T(8,128)(2,1)S(1)} %bitcast.52, f32[2,2048,128,8]{2,1,3,0:T(8,128)S(1)} %get-tuple-element.413, f32[2,8,128]{2,1,0:T(8,128)S(1)} %max.4, pred[128,2048]{0,1:T(8,128)(4,1)S(1)} %bitcast_and_fusion, ...), kind=kOutput, calls=%fused_computation.8 | convolution fusion | flops 2169503744 | bytes 23347200 | tf_op jit(solution)/shard_map/while/body/eval_jaxpr/cond/branch_1_fun/kgrn,nkd->kgrd/dot_general | solution.py:68
  287.6 2.0 divide_bitcast_fusion
  289.8 1.5 multiply_convert_fusion
  (78 shorter events, 16.2 us)
Async XLA Ops:
  6.5 4.4 %copy-start.3 = (s32[1,64]{1,0:T(1,128)S(1)}, s32[1,64]{1,0:T(1,128)}, u32[]{:S(2)}) copy-start(s32[1,64]{1,0:T(1,128)} %param.15) | copy-start | bytes 772
  6.5 46.0 %copy-start.2 = (s32[128]{0:T(128)S(1)}, s32[128]{0:T(128)}, u32[]{:S(2)}) copy-start(s32[128]{0:T(128)} %param.14) | copy-start | bytes 1540
  6.5 88.2 %all-gather.5.cloned.1.call-start = ((), (), s32[]{:S(2)}) async-start(), calls=%async_computation | async-start | bytes 8519680 | tf_op jit(solution)/shard_map/all_gather | solution.py:111
  7.3 170.6 %all-gather.7.cloned.1.call-start = ((), (), s32[]{:S(2)}) async-start(), calls=%async_computation.1 | async-start | bytes 8519680 | tf_op jit(solution)/shard_map/all_gather | solution.py:112
  210.4 2.8 copy-start
  239.8 2.8 copy-start
  269.2 2.8 copy-start
  287.6 2.3 copy-start.1
Sparse Core Ops, SparseCore 0:
  10.1 84.5 all-gather.4
  97.5 80.2 all-gather.6
where the time goes:
time: 299 us; the launch traced here: 298 us
  blocking collectives  78.7 us (26%)
  waiting for transfers between devices  77.8 us (26%)
  local copies, waits for them, and re-layouts  39.7 us (13%)
  matrix products  35 us (12%)
  other arithmetic  34.1 us (11%)
  loops' own time  19.3 us (6%)
  between operations  13.5 us (5%)
    all_gather x1, waiting for transfers between devices, fold_all(): lax.all_gather(value_rows, 'cp', axis=0, tiled=True)  71.6 us
    all_gather x1, blocking collectives, on_device(): lax.all_gather(block_lists, 'cp', axis=0, tiled=True)  41.3 us
    all_gather x1, blocking collectives, on_device(): lax.all_gather(doc_ids, 'cp', axis=0, tiled=True)  37.4 us
    unnamed x11, local copies, waits for them, and re-layouts  26.1 us
    dot_general x3, matrix products, compute(): jnp.einsum('kgrn,nkd->kgrd', weights.astype(jnp.bfloat16), value_block.re...  22.9 us
    another operation x1, loops' own time, fold(): state, _ = lax.scan(advance, state, (key_steps, value_steps, starts))  19.1 us
    reduce_sum x3, other arithmetic, compute(): new_sum = decay * running_sum + jnp.sum(weights, axis=-1)  11.9 us
    dot_general x3, matrix products, compute(): jnp.einsum('rkgd,nkd->kgrn', grouped, key_block.reshape(width, KVH, HD),...  11.9 us
  transfers between devices with their start and end apart: 2, of which 2 were waited for; matrix products, arithmetic and copies ran while one was open for 5% of the time, Pallas kernels for 0%

commit v1 on v0

--- a/solution.py
+++ b/solution.py
@@ -8,6 +8,11 @@
 KVH = 2
 HD = 256
 BLK = 128
+
+
+def gather_from_all(x, axis, dim):
+    copies = jnp.concatenate([x] * lax.axis_size(axis), axis=dim)
+    return lax.all_to_all(copies, axis, dim, dim, tiled=True)
 
 
 def pick_size(length):
@@ -107,10 +112,7 @@
 def fold_all(fold, initial, key_rows, value_rows):
     return fold(
         initial,
-        (
-            lax.all_gather(key_rows, "cp", axis=0, tiled=True),
-            lax.all_gather(value_rows, "cp", axis=0, tiled=True),
-        ),
+        (lax.all_gather(key_rows, "cp", axis=0, tiled=True), gather_from_all(value_rows, "cp", 0)),
         jnp.int32(0),
     )
 

time: 299 us -> 462 us (1.55)
  blocking collectives: 78.7 us -> 273 us
  waiting for transfers between devices: 77.8 us -> 0.68 us
  local copies, waits for them, and re-layouts: 39.7 us -> 71.4 us
  starting transfers between devices: 0.04 us -> 12.8 us
    all_gather x1, blocking collectives: 41.3 us -> 236 us  [on_device(): lax.all_gather(block_lists, 'cp', axis=0, tiled=True)]
    all_gather x1 -> x0, waiting for transfers between devices: 71.6 us -> none  [fold_all(): lax.all_gather(value_rows, 'cp', axis=0, tiled=True)]
    unnamed x11 -> x80, local copies, waits for them, and re-layouts: 26.1 us -> 58.1 us
    all_to_all x0 -> x1, starting transfers between devices: none -> 12.8 us  [gather_from_all(): return lax.all_to_all(copies, axis, dim, dim, tiled=True)]
    all_gather x1, waiting for transfers between devices: 4.77 us -> 0.01 us  [fold_all(): lax.all_gather(key_rows, 'cp', axis=0, tiled=True)]
  transfers between devices with their start and end apart: 2 -> 2, of which waited for: 2 -> 0; matrix products, arithmetic and copies ran while one was open for 5% -> 3% of each run, Pallas kernels for 0% -> 0%
where the time goes in v1:
time: 462 us; the launch traced here: 460 us
  blocking collectives  273 us (59%)
  local copies, waits for them, and re-layouts  71.4 us (15%)
  matrix products  35 us (8%)
  other arithmetic  34.2 us (7%)
  loops' own time  19 us (4%)
  between operations  13.9 us (3%)
  starting transfers between devices  12.8 us (3%)
    all_gather x1, blocking collectives, on_device(): lax.all_gather(block_lists, 'cp', axis=0, tiled=True)  236 us
    unnamed x80, local copies, waits for them, and re-layouts  58.1 us
    all_gather x1, blocking collectives, on_device(): lax.all_gather(doc_ids, 'cp', axis=0, tiled=True)  37 us
    dot_general x3, matrix products, compute(): jnp.einsum('kgrn,nkd->kgrd', weights.astype(jnp.bfloat16), value_block.re...  22.9 us
    another operation x1, loops' own time, fold(): state, _ = lax.scan(advance, state, (key_steps, value_steps, starts))  18.7 us
    all_to_all x1, starting transfers between devices, gather_from_all(): return lax.all_to_all(copies, axis, dim, dim, tiled=True)  12.8 us
    reduce_sum x3, other arithmetic, compute(): new_sum = decay * running_sum + jnp.sum(weights, axis=-1)  11.9 us
    dot_general x3, matrix products, compute(): jnp.einsum('rkgd,nkd->kgrn', grouped, key_block.reshape(width, KVH, HD),...  11.9 us
  transfers between devices with their start and end apart: 2, of which 0 were waited for; matrix products, arithmetic and copies ran while one was open for 3% of the time, Pallas kernels for 0%

profile of v1, /device:TPU:7, one launch (start us, length us, event | category | flops | bytes accessed | tf_op | source)
XLA Modules:
  0.0 460.4 jit_solution(4253824602249291314)
XLA Ops:
  36.6 3.2 copy-done.1
  39.9 12.8 %all-to-all-start = ((bf16[64,128,512]{2,1,0:T(8,128)(2,1)}), bf16[64,128,512]{2,1,0:T(8,128)(2,1)}, u32[]{:S(2)}, u32[]{:S(2)}) async-start(bf16[64,128,512]{2,1,0:T(8,128)(2,1)} %bitcast.55), calls=%async_computation | async-start | bytes 16777216 | tf_op jit(solution)/shard_map/all_to_all | solution.py:15
  55.4 236.3 %all-gather.1 = s32[64,1,64]{2,1,0:T(1,128)S(1)} all-gather(s32[1,1,64]{2,1,0:T(1,128)S(1)} %bitcast.64), channel_id=1, replica_groups=mesh['dp'=4,'cp'=64] {'cp'}, dimensions={0}, use_global_device_ids=true | all-gather | bytes 16640 | tf_op jit(solution)/shard_map/all_gather | solution.py:125
  292.0 37.0 %all-gather = s32[64,1,128]{2,1,0:T(1,128)S(1)} all-gather(s32[1,1,128]{2,1,0:T(1,128)S(1)} %bitcast.62), channel_id=1, replica_groups=mesh['dp'=4,'cp'=64] {'cp'}, dimensions={0}, use_global_device_ids=true | all-gather | bytes 33280 | tf_op jit(solution)/shard_map/all_gather | solution.py:124
  329.0 11.5 %copy.44 = bf16[4,2048,512]{1,2,0:T(8,128)(2,1)} copy(bf16[4,2048,512]{2,1,0:T(8,128)(2,1)} %bitcast.15) | data formatting | bytes 16777216
  340.5 11.5 %copy.42 = bf16[4,2048,512]{1,2,0:T(8,128)(2,1)} copy(bf16[4,2048,512]{2,1,0:T(8,128)(2,1)} %bitcast.56) | data formatting | bytes 16777216
  352.0 1.6 broadcast_in_dim.58
  353.6 96.2 %while.17 = (s32[]{:T(128)}, f32[2,8,128]{2,1,0:T(8,128)S(1)}, f32[2,8,128]{2,1,0:T(8,128)S(1)}, f32[2,8,128,256]{3,2,1,0:T(8,128)}, s32[4]{0:T(128)S(1)}, /*ind...) while((s32[]{:T(128)}, f32[2,8,128]{2,1,0:T(8,128)S(1)}, ...), condition=%wide.region_6.7_spmd.clone, body=%wide.region_0.6_spmd.clone.sunk | while | flops 4353456128 | bytes 73665688 | solution.py:95
  360.0 1.3 and_reduce_fusion.2
  368.4 1.3 and_reduce_fusion.2
  370.3 20.9 %conditional.3 = ((f32[2,8,128]{2,1,0:T(8,128)S(1)}, f32[2,8,128]{2,1,0:T(8,128)S(1)}, f32[2,8,128,256]{3,2,1,0:T(8,128)})) conditional(s32[]{:T(128)} %convert_element_type.42, (f32[2,8,128]{2,1,0:T(8,128)S(1)}, f32[2,8,128]{2,1,0:T(8,128)S(1)}, f32[2,8,128,256]{3,2,1,0:T(8,128)}) %tuple.57, (s32[]{:T(128)}, s32[1,2048]{1,0:T(1,128)S(1)}, ...), branch_computations={%region_2.2_spmd, %region_3.5_spmd} | conditional | flops 4351862784 | bytes 73577536 | solution.py:81
  371.1 1.8 bitcast_and_fusion
  372.9 2.7 constant_dynamic-slice_fusion
  375.6 4.0 fusion.2
  379.6 4.0 fusion.4
  383.6 7.6 %multiply_add_fusion = f32[2,8,128,256]{3,2,1,0:T(8,128)} fusion(f32[2,8,128,256]{3,2,1,0:T(8,128)} %get-tuple-element.282, bf16[2048,2,256,1]{0,2,3,1:T(8,128)(2,1)S(1)} %bitcast.53, f32[2,2048,128,8]{2,1,3,0:T(8,128)S(1)} %get-tuple-element.413, f32[2,8,128]{2,1,0:T(8,128)S(1)} %max.4, pred[128,2048]{0,1:T(8,128)(4,1)S(1)} %bitcast_and_fusion, ...), kind=kOutput, calls=%fused_computation.8 | convolution fusion | flops 2169503744 | bytes 23347200 | tf_op jit(solution)/shard_map/while/body/eval_jaxpr/cond/branch_1_fun/kgrn,nkd->kgrd/dot_general | solution.py:73
  397.6 1.3 and_reduce_fusion.2
  399.6 20.9 %conditional.3 = ((f32[2,8,128]{2,1,0:T(8,128)S(1)}, f32[2,8,128]{2,1,0:T(8,128)S(1)}, f32[2,8,128,256]{3,2,1,0:T(8,128)})) conditional(s32[]{:T(128)} %convert_element_type.42, (f32[2,8,128]{2,1,0:T(8,128)S(1)}, f32[2,8,128]{2,1,0:T(8,128)S(1)}, f32[2,8,128,256]{3,2,1,0:T(8,128)}) %tuple.57, (s32[]{:T(128)}, s32[1,2048]{1,0:T(1,128)S(1)}, ...), branch_computations={%region_2.2_spmd, %region_3.5_spmd} | conditional | flops 4351862784 | bytes 73577536 | solution.py:81
  400.4 1.8 bitcast_and_fusion
  402.2 2.7 constant_dynamic-slice_fusion
  404.8 4.0 fusion.2
  408.8 4.0 fusion.4
  412.8 7.6 %multiply_add_fusion = f32[2,8,128,256]{3,2,1,0:T(8,128)} fusion(f32[2,8,128,256]{3,2,1,0:T(8,128)} %get-tuple-element.282, bf16[2048,2,256,1]{0,2,3,1:T(8,128)(2,1)S(1)} %bitcast.53, f32[2,2048,128,8]{2,1,3,0:T(8,128)S(1)} %get-tuple-element.413, f32[2,8,128]{2,1,0:T(8,128)S(1)} %max.4, pred[128,2048]{0,1:T(8,128)(4,1)S(1)} %bitcast_and_fusion, ...), kind=kOutput, calls=%fused_computation.8 | convolution fusion | flops 2169503744 | bytes 23347200 | tf_op jit(solution)/shard_map/while/body/eval_jaxpr/cond/branch_1_fun/kgrn,nkd->kgrd/dot_general | solution.py:73
  426.9 1.3 and_reduce_fusion.2
  428.8 20.9 %conditional.3 = ((f32[2,8,128]{2,1,0:T(8,128)S(1)}, f32[2,8,128]{2,1,0:T(8,128)S(1)}, f32[2,8,128,256]{3,2,1,0:T(8,128)})) conditional(s32[]{:T(128)} %convert_element_type.42, (f32[2,8,128]{2,1,0:T(8,128)S(1)}, f32[2,8,128]{2,1,0:T(8,128)S(1)}, f32[2,8,128,256]{3,2,1,0:T(8,128)}) %tuple.57, (s32[]{:T(128)}, s32[1,2048]{1,0:T(1,128)S(1)}, ...), branch_computations={%region_2.2_spmd, %region_3.5_spmd} | conditional | flops 4351862784 | bytes 73577536 | solution.py:81
  429.7 1.8 bitcast_and_fusion
  431.4 2.7 constant_dynamic-slice_fusion
  434.1 4.0 fusion.2
  438.1 4.0 fusion.4
  442.1 7.6 %multiply_add_fusion = f32[2,8,128,256]{3,2,1,0:T(8,128)} fusion(f32[2,8,128,256]{3,2,1,0:T(8,128)} %get-tuple-element.282, bf16[2048,2,256,1]{0,2,3,1:T(8,128)(2,1)S(1)} %bitcast.53, f32[2,2048,128,8]{2,1,3,0:T(8,128)S(1)} %get-tuple-element.413, f32[2,8,128]{2,1,0:T(8,128)S(1)} %max.4, pred[128,2048]{0,1:T(8,128)(4,1)S(1)} %bitcast_and_fusion, ...), kind=kOutput, calls=%fused_computation.8 | convolution fusion | flops 2169503744 | bytes 23347200 | tf_op jit(solution)/shard_map/while/body/eval_jaxpr/cond/branch_1_fun/kgrn,nkd->kgrd/dot_general | solution.py:73
  449.7 2.0 divide_bitcast_fusion
  452.0 1.5 multiply_convert_fusion
  (147 shorter events, 44.7 us)
Async XLA Ops:
  6.5 29.5 %copy-start = (bf16[128,512]{1,0:T(8,128)(2,1)S(1)}, bf16[128,512]{1,0:T(8,128)(2,1)}, u32[]{:S(2)}) copy-start(bf16[128,512]{1,0:T(8,128)(2,1)} %param.12) | copy-start | bytes 393220
  36.6 3.2 copy-start.1
  39.9 13.6 %copy-start.2 = (bf16[128,4096]{1,0:T(8,128)(2,1)S(1)}, bf16[128,4096]{1,0:T(8,128)(2,1)}, u32[]{:S(2)}) copy-start(bf16[128,4096]{1,0:T(8,128)(2,1)} %param.10) | copy-start | bytes 3145732
  39.9 15.6 %copy-start.6 = (s32[1,64]{1,0:T(1,128)S(1)}, s32[1,64]{1,0:T(1,128)}, u32[]{:S(2)}) copy-start(s32[1,64]{1,0:T(1,128)} %param.15) | copy-start | bytes 772
  39.9 252.1 %copy-start.5 = (s32[128]{0:T(128)S(1)}, s32[128]{0:T(128)}, u32[]{:S(2)}) copy-start(s32[128]{0:T(128)} %param.14) | copy-start | bytes 1540
  39.9 289.2 %all-to-all-start = ((bf16[64,128,512]{2,1,0:T(8,128)(2,1)}), bf16[64,128,512]{2,1,0:T(8,128)(2,1)}, u32[]{:S(2)}, u32[]{:S(2)}) async-start(bf16[64,128,512]{2,1,0:T(8,128)(2,1)} %bitcast.55), calls=%async_computation | async-start | bytes 16777216 | tf_op jit(solution)/shard_map/all_to_all | solution.py:15
  52.7 287.9 %all-gather.4.cloned.1.call-start = ((), (), s32[]{:S(2)}) async-start(), calls=%async_computation.1 | async-start | bytes 8519680 | tf_op jit(solution)/shard_map/all_gather | solution.py:115
  370.3 5.3 %copy-start.3 = (bf16[128,2,8,256]{3,0,2,1:T(8,128)(2,1)S(1)}, bf16[128,2,8,256]{3,0,2,1:T(8,128)(2,1)}, u32[]{:S(2)}) copy-start(bf16[128,2,8,256]{3,0,2,1:T(8,128)(2,1)} %get-tuple-element.280) | copy-start | bytes 3145732 | tf_op jit(solution)/shard_map/while/body/eval_jaxpr/cond
  399.6 5.3 %copy-start.3 = (bf16[128,2,8,256]{3,0,2,1:T(8,128)(2,1)S(1)}, bf16[128,2,8,256]{3,0,2,1:T(8,128)(2,1)}, u32[]{:S(2)}) copy-start(bf16[128,2,8,256]{3,0,2,1:T(8,128)(2,1)} %get-tuple-element.280) | copy-start | bytes 3145732 | tf_op jit(solution)/shard_map/while/body/eval_jaxpr/cond
  428.8 5.3 %copy-start.3 = (bf16[128,2,8,256]{3,0,2,1:T(8,128)(2,1)S(1)}, bf16[128,2,8,256]{3,0,2,1:T(8,128)(2,1)}, u32[]{:S(2)}) copy-start(bf16[128,2,8,256]{3,0,2,1:T(8,128)(2,1)} %get-tuple-element.280) | copy-start | bytes 3145732 | tf_op jit(solution)/shard_map/while/body/eval_jaxpr/cond
  449.7 2.3 copy-start.4
Sparse Core Ops, SparseCore 0:
  56.3 133.6 all-gather.3
